TPU v7x, 32 devices: a whole 2x2x4 slice. The times are simulated.
32 devices in a mesh: fsdp: 8 (over y, x, core), seq: 4 (over z).
Axes of the slice: x: 2, y: 2, z: 4, core: 2. Of those that a mesh axis runs over, the one named last changes fastest.
Arguments:
- inputs: float32 [4096, 768], P(('fsdp', 'seq')), may hold values from -6 to 6
- qkv_weight: bfloat16 [768, 2304], P(('fsdp', 'seq')), may hold values from -8 to 8
- proj_weight: bfloat16 [768, 768], P(('fsdp', 'seq')), may hold values from -2.5 to 2.5
- first_gain: bfloat16 [768], P(('fsdp', 'seq')), may hold values from 0.5 to 1.5
- first_shift: bfloat16 [768], P(('fsdp', 'seq')), may hold values from -3 to 3
- second_gain: bfloat16 [768], P(('fsdp', 'seq')), may hold values from 0.5 to 1.5
- second_shift: bfloat16 [768], P(('fsdp', 'seq')), may hold values from -3 to 3
- expert_up: bfloat16 [8, 768, 3072], P('fsdp', None, 'seq'), may hold values from -0.21875 to 0.21875
- expert_down: bfloat16 [8, 768, 3072], P('fsdp', None, 'seq'), may hold values from -0.109375 to 0.109375
- gate_logits: float32 [4096, 2], P(('fsdp', 'seq')), may hold values from -160 to 160
- routes: int32 [4096, 2], P(('fsdp', 'seq')), may hold values from 0 to 7, all different within a row; in each aligned block of 128 rows (0 to 127, 128 to 255, ...) at most 64 rows name the same one
- cotangent: float32 [4096, 768], P(('fsdp', 'seq')), may hold values from -6 to 6
Outputs:
- output: float32 [4096, 768], P(('fsdp', 'seq'))
- grad_inputs: float32 [4096, 768], P(('fsdp', 'seq'))
- grad_qkv_weight: float32 [768, 2304], P(('fsdp', 'seq'))
- grad_proj_weight: float32 [768, 768], P(('fsdp', 'seq'))
- grad_first_gain: float32 [768], P(('fsdp', 'seq'))
- grad_first_shift: float32 [768], P(('fsdp', 'seq'))
- grad_second_gain: float32 [768], P(('fsdp', 'seq'))
- grad_second_shift: float32 [768], P(('fsdp', 'seq'))
- grad_expert_up: float32 [8, 768, 3072], P('fsdp', None, 'seq')
- grad_expert_down: float32 [8, 768, 3072], P('fsdp', None, 'seq')
Inputs may be any that keep to these rules, and one draw needn't show every extreme that they name: `routes`: each row names 2 different experts. In each aligned block of 128 rows (the rows of one device) no expert is named by more than 64 rows, a bound that some block reaches.
All inputs are finite; a program needn't handle non-finite values.
Results may differ from a plain program's by a relative error of at most 0.012.
Values may be sent and summed in bfloat16 or wider, within the bound.
No kernel may reach another device: no remote copies, remote signals or barrier semaphores. Data moves between devices by JAX's collectives and lax.ppermute only.
A program may use at most 128 MiB of HBM per device.

v0:
```python
import jax
import jax.numpy as jnp
from jax import lax
from jax.sharding import PartitionSpec as P

HD = 64
epsilon = 1e-06


def layer_norm(rows_in, gain_row, shift_row):
    average = jnp.mean(rows_in, axis=-1, keepdims=True)
    centred = rows_in - average
    spread = jnp.mean(centred * centred, axis=-1, keepdims=True)
    return centred * lax.rsqrt(spread + epsilon) * gain_row + shift_row


def attention_forward(q_rows, k_rows, v_rows):
    length = q_rows.shape[0]
    block_rows = min(512, length)
    score_scale = q_rows.shape[2] ** (-0.5)
    grouped = q_rows.reshape(length // block_rows, block_rows, q_rows.shape[1], q_rows.shape[2])

    def one_block(q_block):
        scores = (
            jnp.einsum("qhd,khd->hqk", q_block, k_rows, preferred_element_type=jnp.float32)
            * score_scale
        )
        top_score = jnp.max(scores, axis=-1, keepdims=True)
        weights = jnp.exp(scores - top_score)
        totals = jnp.sum(weights, axis=-1, keepdims=True)
        probs_low = (weights / totals).astype(jnp.bfloat16)
        result = jnp.einsum(
            "hqk,khd->qhd", probs_low, v_rows, preferred_element_type=jnp.float32
        ).astype(jnp.bfloat16)
        return (result, (top_score + jnp.log(totals))[..., 0])

    results, log_totals = lax.map(one_block, grouped)
    return (results.reshape(q_rows.shape), log_totals)


def attention_backward(q_rows, k_rows, v_rows, log_totals, grad_out):
    length = q_rows.shape[0]
    block_rows = min(512, length)
    score_scale = q_rows.shape[2] ** (-0.5)
    grouped_q = q_rows.reshape(length // block_rows, block_rows, q_rows.shape[1], q_rows.shape[2])
    grouped_g = grad_out.reshape(grouped_q.shape)

    def one_block(running, pieces):
        grad_k, grad_v = running
        q_block, g_block, lse_block = pieces
        scores = (
            jnp.einsum("qhd,khd->hqk", q_block, k_rows, preferred_element_type=jnp.float32)
            * score_scale
        )
        probs_full = jnp.exp(scores - lse_block[..., None])
        probs_low = probs_full.astype(jnp.bfloat16)
        grad_v = grad_v + jnp.einsum(
            "hqk,qhd->khd", probs_low, g_block, preferred_element_type=jnp.float32
        )
        grad_p = jnp.einsum("qhd,khd->hqk", g_block, v_rows, preferred_element_type=jnp.float32)
        row_dot = jnp.sum(probs_full * grad_p, axis=-1, keepdims=True)
        grad_s = (probs_full * (grad_p - row_dot) * score_scale).astype(jnp.bfloat16)
        grad_q = jnp.einsum(
            "hqk,khd->qhd", grad_s, k_rows, preferred_element_type=jnp.float32
        ).astype(jnp.bfloat16)
        grad_k = grad_k + jnp.einsum(
            "hqk,qhd->khd", grad_s, q_block, preferred_element_type=jnp.float32
        )
        return ((grad_k, grad_v), grad_q)

    empty_grad = jnp.zeros(k_rows.shape, jnp.float32)
    (grad_k, grad_v), grad_q = lax.scan(
        one_block, (empty_grad, empty_grad), (grouped_q, grouped_g, log_totals)
    )
    return (grad_q.reshape(q_rows.shape), grad_k.astype(jnp.bfloat16), grad_v.astype(jnp.bfloat16))


def slot_table(routes, experts, capacity):
    flat_ids = routes.reshape(-1)
    labels = jnp.arange(experts, dtype=jnp.int32)
    onehot = (flat_ids[:, None] == labels[None, :]).astype(jnp.int32)
    before = jnp.cumsum(onehot, axis=0) - onehot
    return flat_ids * capacity + jnp.sum(before * onehot, axis=1)


def place_rows(entries, slot_ids, slot_count):
    return jnp.zeros((slot_count, entries.shape[1]), entries.dtype).at[slot_ids].set(entries)


def expert_forward(rows_in, up_mat, down_mat):
    pre_act = jnp.dot(rows_in, up_mat, preferred_element_type=jnp.float32)
    hidden = jax.nn.gelu(pre_act).astype(jnp.bfloat16)
    result = lax.dot_general(
        hidden, down_mat, (((1,), (1,)), ((), ())), preferred_element_type=jnp.float32
    )
    return (pre_act, hidden, result)


def expert_backward(rows_in, pre_act, hidden, grad_out, up_mat, down_mat):
    grad_hidden = jnp.dot(grad_out, down_mat, preferred_element_type=jnp.float32)
    _, gelu_back = jax.vjp(jax.nn.gelu, pre_act)
    grad_pre = gelu_back(grad_hidden)[0].astype(jnp.bfloat16)
    grad_down = lax.dot_general(
        grad_out, hidden, (((0,), (0,)), ((), ())), preferred_element_type=jnp.float32
    )
    grad_up = lax.dot_general(
        rows_in, grad_pre, (((0,), (0,)), ((), ())), preferred_element_type=jnp.float32
    )
    grad_rows = lax.dot_general(
        grad_pre, up_mat, (((1,), (1,)), ((), ())), preferred_element_type=jnp.float32
    )
    return (grad_rows, grad_up, grad_down)


def to_experts(buffer):
    return lax.all_to_all(buffer, "fsdp", split_axis=0, concat_axis=0, tiled=True)


def from_experts(buffer):
    return lax.all_to_all(buffer, "fsdp", split_axis=0, concat_axis=0, tiled=True)


def local(
    inputs,
    qkv_weight,
    proj_weight,
    first_gain,
    first_shift,
    second_gain,
    second_shift,
    expert_up,
    expert_down,
    gate_logits,
    routes,
    cotangent,
):
    tok_count, model_width = inputs.shape
    seq_count = lax.axis_size("seq")
    experts = lax.axis_size("fsdp")
    top_count = routes.shape[1]
    capacity = 4 * tok_count // experts
    slot_count = experts * capacity
    seq_len = tok_count * seq_count
    group_width = model_width // seq_count
    group_heads = group_width // HD
    qkv_full, proj_full, gain_one, shift_one, gain_two, shift_two = (
        lax.all_gather(qkv_weight, ("fsdp", "seq"), axis=0, tiled=True),
        lax.all_gather(proj_weight, ("fsdp", "seq"), axis=0, tiled=True),
        lax.all_gather(first_gain, ("fsdp", "seq"), axis=0, tiled=True),
        lax.all_gather(first_shift, ("fsdp", "seq"), axis=0, tiled=True),
        lax.all_gather(second_gain, ("fsdp", "seq"), axis=0, tiled=True),
        lax.all_gather(second_shift, ("fsdp", "seq"), axis=0, tiled=True),
    )
    gain_one = gain_one.astype(jnp.float32)
    shift_one = shift_one.astype(jnp.float32)
    gain_two = gain_two.astype(jnp.float32)
    shift_two = shift_two.astype(jnp.float32)
    attn_in = layer_norm(inputs, gain_one, shift_one).astype(jnp.bfloat16)
    qkv_rows = jnp.dot(attn_in, qkv_full, preferred_element_type=jnp.float32).astype(jnp.bfloat16)
    qkv_group = lax.all_to_all(
        qkv_rows.reshape(tok_count, 3, seq_count, group_width),
        "seq",
        split_axis=2,
        concat_axis=0,
        tiled=True,
    )
    q_rows = qkv_group[:, 0, 0].reshape(seq_len, group_heads, HD)
    k_rows = qkv_group[:, 1, 0].reshape(seq_len, group_heads, HD)
    v_rows = qkv_group[:, 2, 0].reshape(seq_len, group_heads, HD)
    heads_local, log_totals = attention_forward(q_rows, k_rows, v_rows)
    heads_out = lax.all_to_all(
        heads_local.reshape(seq_len, 1, group_width), "seq", split_axis=0, concat_axis=1, tiled=True
    ).reshape(tok_count, model_width)
    residual = inputs + jnp.dot(heads_out, proj_full, preferred_element_type=jnp.float32)
    ffn_in = layer_norm(residual, gain_two, shift_two).astype(jnp.bfloat16)
    top_logit = jnp.max(gate_logits, axis=1, keepdims=True)
    raised = jnp.exp(gate_logits - top_logit)
    gate_probs = raised / jnp.sum(raised, axis=1, keepdims=True)
    slot_ids = slot_table(routes, experts, capacity)
    sent = place_rows(jnp.repeat(ffn_in, top_count, axis=0), slot_ids, slot_count)
    arrived = to_experts(sent.reshape(experts, capacity, model_width))
    grad_entry = (
        (gate_probs[:, :, None] * cotangent[:, None, :])
        .astype(jnp.bfloat16)
        .reshape(tok_count * top_count, model_width)
    )
    grad_arrived = to_experts(
        place_rows(grad_entry, slot_ids, slot_count).reshape(experts, capacity, model_width)
    )
    up_full, down_full = (
        lax.all_gather(expert_up, "seq", axis=2, tiled=True),
        lax.all_gather(expert_down, "seq", axis=2, tiled=True),
    )
    rows_in = arrived.reshape(-1, model_width)
    pre_act, hidden, produced = expert_forward(rows_in, up_full[0], down_full[0])
    expert_out = produced.astype(jnp.bfloat16)
    grad_part, grad_up, grad_down = expert_backward(
        rows_in, pre_act, hidden, grad_arrived.reshape(-1, model_width), up_full[0], down_full[0]
    )
    grad_rows = grad_part.astype(jnp.bfloat16)
    grad_expert_up, grad_expert_down = (
        lax.psum_scatter(
            grad_up[None].astype(jnp.bfloat16), "seq", scatter_dimension=2, tiled=True
        ).astype(jnp.float32),
        lax.psum_scatter(
            grad_down[None].astype(jnp.bfloat16), "seq", scatter_dimension=2, tiled=True
        ).astype(jnp.float32),
    )
    returned = from_experts(expert_out.reshape(experts, capacity, model_width)).reshape(
        slot_count, model_width
    )
    picked = returned[slot_ids].reshape(tok_count, top_count, model_width)
    output = residual + jnp.sum(gate_probs[:, :, None] * picked.astype(jnp.float32), axis=1)
    grad_back = from_experts(grad_rows.reshape(experts, capacity, model_width)).reshape(
        slot_count, model_width
    )
    grad_ffn_in = jnp.sum(
        grad_back[slot_ids].reshape(tok_count, top_count, model_width).astype(jnp.float32), axis=1
    )
    _, second_back = jax.vjp(layer_norm, residual, gain_two, shift_two)
    grad_from_ffn, grad_gain_two, grad_shift_two = second_back(grad_ffn_in)
    grad_residual = cotangent + grad_from_ffn
    grad_mix = grad_residual.astype(jnp.bfloat16)
    grad_proj = lax.dot_general(
        heads_out, grad_mix, (((0,), (0,)), ((), ())), preferred_element_type=jnp.float32
    )
    grad_heads = lax.dot_general(
        grad_mix, proj_full, (((1,), (1,)), ((), ())), preferred_element_type=jnp.float32
    ).astype(jnp.bfloat16)
    grad_group = lax.all_to_all(
        grad_heads.reshape(tok_count, seq_count, group_width),
        "seq",
        split_axis=1,
        concat_axis=0,
        tiled=True,
    ).reshape(seq_len, group_heads, HD)
    grad_q, grad_k, grad_v = attention_backward(q_rows, k_rows, v_rows, log_totals, grad_group)
    stacked = jnp.stack([grad_q, grad_k, grad_v], axis=1).reshape(seq_len, 3, 1, group_width)
    grad_qkv = lax.all_to_all(stacked, "seq", split_axis=0, concat_axis=2, tiled=True).reshape(
        tok_count, 3 * model_width
    )
    grad_qkv_part = lax.dot_general(
        attn_in, grad_qkv, (((0,), (0,)), ((), ())), preferred_element_type=jnp.float32
    )
    grad_attn_in = lax.dot_general(
        grad_qkv, qkv_full, (((1,), (1,)), ((), ())), preferred_element_type=jnp.float32
    )
    _, first_back = jax.vjp(layer_norm, inputs, gain_one, shift_one)
    grad_from_attn, grad_gain_one, grad_shift_one = first_back(grad_attn_in)
    grad_inputs = grad_residual + grad_from_attn
    reduced = (
        lax.psum_scatter(grad_qkv_part, ("fsdp", "seq"), scatter_dimension=0, tiled=True),
        lax.psum_scatter(grad_proj, ("fsdp", "seq"), scatter_dimension=0, tiled=True),
        lax.psum_scatter(grad_gain_one, ("fsdp", "seq"), scatter_dimension=0, tiled=True),
        lax.psum_scatter(grad_shift_one, ("fsdp", "seq"), scatter_dimension=0, tiled=True),
        lax.psum_scatter(grad_gain_two, ("fsdp", "seq"), scatter_dimension=0, tiled=True),
        lax.psum_scatter(grad_shift_two, ("fsdp", "seq"), scatter_dimension=0, tiled=True),
    )
    return (
        output,
        grad_inputs,
        reduced[0],
        reduced[1],
        reduced[2],
        reduced[3],
        reduced[4],
        reduced[5],
        grad_expert_up,
        grad_expert_down,
    )


def solution(mesh):
    in_specs = (
        P(("fsdp", "seq"), None),
        P(("fsdp", "seq"), None),
        P(("fsdp", "seq"), None),
        P(("fsdp", "seq")),
        P(("fsdp", "seq")),
        P(("fsdp", "seq")),
        P(("fsdp", "seq")),
        P("fsdp", None, "seq"),
        P("fsdp", None, "seq"),
        P(("fsdp", "seq"), None),
        P(("fsdp", "seq"), None),
        P(("fsdp", "seq"), None),
    )
    out_specs = (
        P(("fsdp", "seq"), None),
        P(("fsdp", "seq"), None),
        P(("fsdp", "seq"), None),
        P(("fsdp", "seq"), None),
        P(("fsdp", "seq")),
        P(("fsdp", "seq")),
        P(("fsdp", "seq")),
        P(("fsdp", "seq")),
        P("fsdp", None, "seq"),
        P("fsdp", None, "seq"),
    )
    return jax.shard_map(local, mesh=mesh, in_specs=in_specs, out_specs=out_specs, check_vma=False)
```

profile of v0, /device:TPU:0, one launch (start us, length us, event | category | flops | bytes accessed | tf_op | source)
XLA Modules:
  0.0 763.2 jit_solution(16794710249775724188)
XLA Ops:
  13.4 42.3 %all-reduce.9 = (bf16[768]{0:T(1024)(128)(2,1)S(1)}, bf16[768]{0:T(1024)(128)(2,1)S(1)}, bf16[768]{0:T(1024)(128)(2,1)S(1)}, bf16[768]{0:T(1024)(128)(2,1)S(1)}) all-reduce(bf16[768]{0:T(1024)(128)(2,1)S(1)} %dynamic-update-slice.1, bf16[768]{0:T(1024)(128)(2,1)S(1)} %dynamic-update-slice, ...), channel_id=1, replica_groups=mesh['fsdp'=8,'seq'=4] {'fsdp','seq'}, use_global_device_ids=true, to_apply=%add.1 | all-reduce | flops 3072 | bytes 12288
  57.1 16.5 %all-gather.5.cloned.1.call-done = bf16[768,2304]{1,0:T(8,128)(2,1)} async-done(((bf16[24,2304]{1,0:T(8,128)(2,1)}), bf16[768,2304]{1,0:T(8,128)(2,1)}) %all-gather.5.cloned.1.call-update) | async-done | bytes 3538960 | tf_op jit(solution)/shard_map/all_gather | solution.py:147
  85.4 12.9 %all-to-all-done = bf16[128,3,4,192]{0,3,1,2:T(8,128)(2,1)S(1)} async-done(((bf16[128,3,4,192]{0,3,1,2:T(8,128)(2,1)}), bf16[128,3,4,192]{0,3,1,2:T(8,128)(2,1)S(1)}, u32[]{:S(2)}, u32[]{:S(2)}) %all-to-all-start) | async-done | bytes 589856 | tf_op jit(solution)/shard_map/all_to_all | solution.py:160
  114.3 5.6 all-to-all-done.1
  127.1 7.7 %all-gather.7.cloned.1.call-done = bf16[768,768]{1,0:T(8,128)(2,1)} async-done(((bf16[24,768]{1,0:T(8,128)(2,1)}), bf16[768,768]{1,0:T(8,128)(2,1)}) %all-gather.7.cloned.1.call-update) | async-done | bytes 1179664 | tf_op jit(solution)/shard_map/all_gather | solution.py:148
  163.0 14.7 %all-to-all-start.4 = ((bf16[8,64,768]{2,1,0:T(8,128)(2,1)}), bf16[8,64,768]{2,1,0:T(8,128)(2,1)}, u32[]{:S(2)}, u32[]{:S(2)}) async-start(bf16[8,64,768]{2,1,0:T(8,128)(2,1)} %bitcast.103), calls=%async_computation.4 | async-start | bytes 1572864 | tf_op jit(solution)/shard_map/all_to_all | solution.py:116
  177.8 46.9 %all-gather.9.cloned.1.call-done = bf16[1,768,3072]{2,1,0:T(8,128)(2,1)} async-done(((bf16[1,768,768]{2,1,0:T(8,128)(2,1)}), bf16[1,768,3072]{2,1,0:T(8,128)(2,1)}) %all-gather.9.cloned.1.call-update) | async-done | bytes 4718608 | tf_op jit(solution)/shard_map/all_gather | solution.py:191
  224.7 8.0 %fusion.14 = f32[512,3072]{1,0:T(8,128)} fusion(bf16[512,768]{1,0:T(8,128)(2,1)} %bitcast.15, bf16[1,768,3072]{2,1,0:T(8,128)(2,1)} %all-gather.9.cloned.1.call-done), kind=kOutput, calls=%fused_computation.23 | convolution fusion | flops 2415919104 | bytes 11796480 | tf_op jit(solution)/shard_map/dot_general | solution.py:91
  232.7 81.2 %all-gather.11.cloned.1.call-done = bf16[1,768,3072]{2,1,0:T(8,128)(2,1)} async-done(((bf16[1,768,768]{2,1,0:T(8,128)(2,1)}), bf16[1,768,3072]{2,1,0:T(8,128)(2,1)}) %all-gather.11.cloned.1.call-update) | async-done | bytes 4718608 | tf_op jit(solution)/shard_map/all_gather | solution.py:192
  313.9 8.5 %fusion.7 = bf16[512,3072]{1,0:T(8,128)(2,1)S(1)} fusion(f32[512,3072]{1,0:T(8,128)} %fusion.14, bf16[512,768]{1,0:T(8,128)(2,1)} %bitcast.21, bf16[1,768,3072]{2,1,0:T(8,128)(2,1)} %all-gather.11.cloned.1.call-done), kind=kOutput, calls=%fused_computation.13 | convolution fusion | flops 2447376384 | bytes 14942208 | tf_op jit(solution)/shard_map/dot_general | solution.py:100
  324.1 5.5 fusion.16
  329.7 8.1 %fusion.17 = bf16[1,768,3072]{2,1,0:T(8,128)(2,1)} fusion(bf16[512,768]{1,0:T(8,128)(2,1)} %bitcast.21, f32[512,3072]{1,0:T(8,128)} %fusion.14), kind=kOutput, calls=%fused_computation.26 | convolution fusion | flops 2432434176 | bytes 11796480 | tf_op jit(solution)/shard_map/dot_general | solution.py:103
  337.8 8.8 %fusion.38 = bf16[512,768]{1,0:T(8,128)(2,1)} fusion(bf16[1,768,3072]{2,1,0:T(8,128)(2,1)} %all-gather.11.cloned.1.call-done, f32[512,3072]{1,0:T(8,128)} %fusion.14), kind=kOutput, calls=%fused_computation.44 | convolution fusion | flops 2430468096 | bytes 11796480 | tf_op jit(solution)/shard_map/dot_general | solution.py:93
  350.9 6.8 fusion.35
  357.7 5.8 all-to-all-done.3
  363.4 4.2 all-to-all-start.5
  372.7 7.6 all-to-all-done.5
  410.8 5.9 all-to-all-done.6
  427.9 5.2 fusion.45
  435.0 5.3 fusion.48
  444.8 56.4 %all_to_all.83 = bf16[512,3,1,192]{3,1,2,0:T(4,128)(2,1)S(1)} all-to-all(bf16[512,3,1,192]{3,1,2,0:T(4,128)(2,1)S(1)} %pad_maximum_fusion), channel_id=1, replica_groups=mesh['fsdp'=8,'seq'=4] {'seq'}, dimensions={0} | all-to-all | bytes 1179648 | tf_op jit(solution)/shard_map/all_to_all | solution.py:239
  511.5 39.6 %all-reduce.8 = (f32[768]{0:T(1024)S(1)}, f32[768]{0:T(1024)S(1)}, f32[768]{0:T(1024)S(1)}, f32[768]{0:T(1024)S(1)}) all-reduce(f32[768]{0:T(1024)S(1)} %get-tuple-element.48, f32[768]{0:T(1024)S(1)} %get-tuple-element.50, f32[768]{0:T(1024)S(1)} %copy-done.15, ...), channel_id=4, replica_groups=mesh['fsdp'=8,'seq'=4] {'fsdp','seq'}, use_global_device_ids=true, to_apply=%region_23.24.clone | all-reduce | flops 3072 | bytes 24576
  560.3 70.9 %reduce-scatter.7.cloned.1.call-done = f32[24,768]{1,0:T(8,128)} async-done(((f32[768,768]{1,0:T(8,128)}), f32[24,768]{1,0:T(8,128)}) %reduce-scatter.7.cloned.1.call-update) | async-done | bytes 73744 | tf_op jit(solution)/shard_map/reduce_scatter | solution.py:253
  631.2 124.8 %reduce-scatter.5.cloned.1.call-done = f32[24,2304]{1,0:T(8,128)} async-done(((f32[768,2304]{1,0:T(8,128)}), f32[24,2304]{1,0:T(8,128)}) %reduce-scatter.5.cloned.1.call-update) | async-done | bytes 221200 | tf_op jit(solution)/shard_map/reduce_scatter | solution.py:252
  (175 shorter events, 148.7 us)
Async XLA Ops:
  7.2 49.7 %copy-start = (f32[128,768]{1,0:T(8,128)S(1)}, f32[128,768]{1,0:T(8,128)}, u32[]{:S(2)}) copy-start(f32[128,768]{1,0:T(8,128)} %param.12) | copy-start | bytes 1179652
  7.2 66.5 %all-gather.5.cloned.1.call-start = ((), (), s32[]{:S(2)}) async-start(), calls=%async_computation.12 | async-start | bytes 3649536 | tf_op jit(solution)/shard_map/all_gather | solution.py:147
  7.9 126.9 %all-gather.7.cloned.1.call-start = ((), (), s32[]{:S(2)}) async-start(), calls=%async_computation.13 | async-start | bytes 1216512 | tf_op jit(solution)/shard_map/all_gather | solution.py:148
  8.7 216.0 %all-gather.9.cloned.1.call-start = ((), (), s32[]{:S(2)}) async-start(), calls=%async_computation.14 | async-start | bytes 5898240 | tf_op jit(solution)/shard_map/all_gather | solution.py:191
  9.4 304.5 %all-gather.11.cloned.1.call-start = ((), (), s32[]{:S(2)}) async-start(), calls=%async_computation.15 | async-start | bytes 5898240 | tf_op jit(solution)/shard_map/all_gather | solution.py:192
  56.9 16.8 %copy-start.13 = (f32[128]{0:T(128)}, f32[128]{0:T(128)S(1)}, u32[]{:S(2)}) copy-start(f32[128]{0:T(128)S(1)} %broadcast_multiply_fusion.2) | copy-start | bytes 1540
  57.1 16.6 %copy-start.21 = (f32[128]{0:T(128)}, f32[128]{0:T(128)S(1)}, u32[]{:S(2)}) copy-start(f32[128]{0:T(128)S(1)} %multiply_reduce_fusion.8) | copy-start | bytes 1540
  57.1 16.6 %copy-start.16 = (f32[128]{0:T(128)}, f32[128]{0:T(128)S(1)}, u32[]{:S(2)}) copy-start(f32[128]{0:T(128)S(1)} %fusion.66) | copy-start | bytes 1540
  57.1 23.9 %copy-start.20 = (s32[128,2]{0,1:T(2,128)S(1)}, s32[128,2]{0,1:T(2,128)}, u32[]{:S(2)}) copy-start(s32[128,2]{0,1:T(2,128)} %param.22) | copy-start | bytes 3076
  77.5 20.8 %all-to-all-start = ((bf16[128,3,4,192]{0,3,1,2:T(8,128)(2,1)}), bf16[128,3,4,192]{0,3,1,2:T(8,128)(2,1)S(1)}, u32[]{:S(2)}, u32[]{:S(2)}) async-start(bf16[128,3,4,192]{0,3,1,2:T(8,128)(2,1)} %copy.60), calls=%async_computation | async-start | bytes 1179648 | tf_op jit(solution)/shard_map/all_to_all | solution.py:160
  108.4 11.6 %all-to-all-start.1 = ((bf16[4,2,12288]{2,1,0:T(2,128)(2,1)}), bf16[4,2,12288]{2,1,0:T(2,128)(2,1)}, u32[]{:S(2)}, u32[]{:S(2)}) async-start(bf16[4,2,12288]{2,1,0:T(2,128)(2,1)} %reshape.275), calls=%async_computation.1 | async-start | bytes 393216 | tf_op jit(solution)/shard_map/all_to_all | solution.py:171
  144.6 18.3 %all-to-all-start.2 = ((bf16[8,64,768]{2,1,0:T(8,128)(2,1)}), bf16[8,64,768]{2,1,0:T(8,128)(2,1)}, u32[]{:S(2)}, u32[]{:S(2)}) async-start(bf16[8,64,768]{2,1,0:T(8,128)(2,1)} %bitcast.102), calls=%async_computation.2 | async-start | bytes 1572864 | tf_op jit(solution)/shard_map/all_to_all | solution.py:116
  163.0 69.7 %all-to-all-start.4 = ((bf16[8,64,768]{2,1,0:T(8,128)(2,1)}), bf16[8,64,768]{2,1,0:T(8,128)(2,1)}, u32[]{:S(2)}, u32[]{:S(2)}) async-start(bf16[8,64,768]{2,1,0:T(8,128)(2,1)} %bitcast.103), calls=%async_computation.4 | async-start | bytes 1572864 | tf_op jit(solution)/shard_map/all_to_all | solution.py:116
  177.7 376.8 %reduce-scatter.9.cloned.1.call-start = ((), (), s32[]{:S(2)}) async-start(), calls=%async_computation.18 | async-start | bytes 5898240 | tf_op jit(solution)/shard_map/reduce_scatter | solution.py:202
  329.6 227.8 %reduce-scatter.11.cloned.1.call-start = ((), (), s32[]{:S(2)}) async-start(), calls=%async_computation.19 | async-start | bytes 5898240 | tf_op jit(solution)/shard_map/reduce_scatter | solution.py:205
  346.7 16.8 %all-to-all-start.3 = ((bf16[8,64,768]{2,1,0:T(8,128)(2,1)}), bf16[8,64,768]{2,1,0:T(8,128)(2,1)}, u32[]{:S(2)}, u32[]{:S(2)}) async-start(bf16[8,64,768]{2,1,0:T(8,128)(2,1)} %bitcast.115), calls=%async_computation.3 | async-start | bytes 1572864 | tf_op jit(solution)/shard_map/all_to_all | solution.py:120
  363.4 16.8 %all-to-all-start.5 = ((bf16[8,64,768]{2,1,0:T(8,128)(2,1)}), bf16[8,64,768]{2,1,0:T(8,128)(2,1)}, u32[]{:S(2)}, u32[]{:S(2)}) async-start(bf16[8,64,768]{2,1,0:T(8,128)(2,1)} %bitcast.114), calls=%async_computation.5 | async-start | bytes 1572864 | tf_op jit(solution)/shard_map/all_to_all | solution.py:120
  367.7 263.5 %reduce-scatter.7.cloned.1.call-start = ((), (), s32[]{:S(2)}) async-start(), calls=%async_computation.17 | async-start | bytes 2433024 | tf_op jit(solution)/shard_map/reduce_scatter | solution.py:253
  405.2 11.5 %all-to-all-start.6 = ((bf16[128,4,192]{0,2,1:T(8,128)(2,1)}), bf16[128,4,192]{0,2,1:T(8,128)(2,1)}, u32[]{:S(2)}, u32[]{:S(2)}) async-start(bf16[128,4,192]{0,2,1:T(8,128)(2,1)} %bitcast.116), calls=%async_computation.6 | async-start | bytes 393216 | tf_op jit(solution)/shard_map/all_to_all | solution.py:230
  409.2 346.8 %reduce-scatter.5.cloned.1.call-start = ((), (), s32[]{:S(2)}) async-start(), calls=%async_computation.16 | async-start | bytes 7299072 | tf_op jit(solution)/shard_map/reduce_scatter | solution.py:252
  441.6 61.2 %copy-start.14 = (f32[128]{0:T(128)S(1)}, f32[128]{0:T(128)}, u32[]{:S(2)}) copy-start(f32[128]{0:T(128)} %copy-done.13) | copy-start | bytes 1540
  441.6 61.2 %copy-start.17 = (f32[128]{0:T(128)S(1)}, f32[128]{0:T(128)}, u32[]{:S(2)}) copy-start(f32[128]{0:T(128)} %copy-done.16) | copy-start | bytes 1540
  506.9 46.5 %copy-start.22 = (f32[128]{0:T(128)S(1)}, f32[128]{0:T(128)}, u32[]{:S(2)}) copy-start(f32[128]{0:T(128)} %copy-done.21) | copy-start | bytes 1540
  508.0 45.7 %copy-start.3 = (f32[128,768]{1,0:T(8,128)S(1)}, f32[128,768]{1,0:T(8,128)}, u32[]{:S(2)}) copy-start(f32[128,768]{1,0:T(8,128)} %copy-done.2) | copy-start | bytes 1179652
  (16 other events, 52.2 us)
Sparse Core Ops, SparseCore 0:
  10.8 62.8 all-gather.4
  76.5 58.2 all-gather.6
  136.4 88.2 all-gather.8
  226.1 87.7 all-gather.10
  329.8 84.7 reduce-scatter.8
  416.7 104.2 reduce-scatter.10
  526.8 104.2 reduce-scatter.6
  637.4 118.5 reduce-scatter.4
where the time goes:
time: 774 us; the launch traced here: 763 us
  waiting for transfers between devices  388 us (50%)
  blocking collectives  138 us (18%)
  matrix products  80.9 us (10%)
  local copies, waits for them, and re-layouts  63 us (8%)
  starting transfers between devices  39.6 us (5%)
  other arithmetic  37.9 us (5%)
  between operations  15.1 us (2%)
    reduce_scatter x1, waiting for transfers between devices, local(): lax.psum_scatter(grad_qkv_part, ('fsdp', 'seq'), scatter_dimension=0, til...  125 us
    unnamed x2, blocking collectives  81.9 us
    all_gather x1, waiting for transfers between devices, local(): lax.all_gather(expert_down, 'seq', axis=2, tiled=True)  81.2 us
    reduce_scatter x1, waiting for transfers between devices, local(): lax.psum_scatter(grad_proj, ('fsdp', 'seq'), scatter_dimension=0, tiled=T...  70.9 us
    all_to_all x1, blocking collectives, local(): lax.all_to_all(stacked, 'seq', split_axis=0, concat_axis=2, tiled=True)  56.4 us
    all_gather x1, waiting for transfers between devices, local(): lax.all_gather(expert_up, 'seq', axis=2, tiled=True)  46.9 us
    all_to_all x2, starting transfers between devices, to_experts(): lax.all_to_all(buffer, 'fsdp', split_axis=0, concat_axis=0, tiled=True)  18.9 us
    unnamed x66, local copies, waits for them, and re-layouts  16.6 us
  transfers between devices with their start and end apart: 15, of which 11 were waited for; matrix products, arithmetic and copies ran while one was open for 21% of the time, Pallas kernels for 0%

commit v1 on v0

--- a/solution.py
+++ b/solution.py
@@ -5,6 +5,27 @@
 
 HD = 64
 epsilon = 1e-06
+
+
+def gather_around(array, axis, dim):
+    devices, index, rows = (lax.axis_size(axis), lax.axis_index(axis), array.shape[dim])
+    right = [(i, (i + 1) % devices) for i in range(devices)]
+    left = [(i, (i - 1) % devices) for i in range(devices)]
+    whole = jnp.zeros((*array.shape[:dim], devices * rows, *array.shape[dim + 1 :]), array.dtype)
+    whole = lax.dynamic_update_slice_in_dim(whole, array, index * rows, axis=dim)
+    from_left = from_right = array
+    middle = devices // 2
+    for lap in range(1, middle + 1):
+        from_left = lax.ppermute(from_left, axis, right)
+        whole = lax.dynamic_update_slice_in_dim(
+            whole, from_left, (index - lap) % devices * rows, axis=dim
+        )
+        if lap < devices - middle:
+            from_right = lax.ppermute(from_right, axis, left)
+            whole = lax.dynamic_update_slice_in_dim(
+                whole, from_right, (index + lap) % devices * rows, axis=dim
+            )
+    return whole
 
 
 def layer_norm(rows_in, gain_row, shift_row):
@@ -189,7 +210,7 @@
     )
     up_full, down_full = (
         lax.all_gather(expert_up, "seq", axis=2, tiled=True),
-        lax.all_gather(expert_down, "seq", axis=2, tiled=True),
+        gather_around(expert_down, "seq", 2),
     )
     rows_in = arrived.reshape(-1, model_width)
     pre_act, hidden, produced = expert_forward(rows_in, up_full[0], down_full[0])

time: 774 us -> 726 us (0.938)
  waiting for transfers between devices: 388 us -> 306 us
  blocking collectives: 138 us -> 171 us
  local copies, waits for them, and re-layouts: 63 us -> 71.6 us
    all_gather x1 -> x0, waiting for transfers between devices: 81.2 us -> none  [local(): lax.all_gather(expert_down, 'seq', axis=2, tiled=True)]
    unnamed x2, blocking collectives: 81.9 us -> 114 us
    all_gather x1, waiting for transfers between devices: 7.73 us -> 25 us  [local(): lax.all_gather(proj_weight, ('fsdp', 'seq'), axis=0, tiled=True)]
    all_gather x1, waiting for transfers between devices: 16.5 us -> 0.02 us  [local(): lax.all_gather(qkv_weight, ('fsdp', 'seq'), axis=0, tiled=True)]
    all_to_all x2, starting transfers between devices: 18.9 us -> 8.89 us  [to_experts(): lax.all_to_all(buffer, 'fsdp', split_axis=0, concat_axis=0, tiled=True)]
    dynamic_update_slice x0 -> x4, local copies, waits for them, and re-layouts: none -> 8.52 us  [the longest x2 4.94 us: gather_around(): lax.dynamic_update_slice_in_dim(whole, from_left, (index - lap) % devices...]
    unnamed x66 -> x70, local copies, waits for them, and re-layouts: 16.6 us -> 15.7 us
  transfers between devices with their start and end apart: 15 -> 17, of which waited for: 11 -> 8; matrix products, arithmetic and copies ran while one was open for 21% -> 23% of each run, Pallas kernels for 0% -> 0%
where the time goes in v1:
time: 726 us; the launch traced here: 717 us
  waiting for transfers between devices  306 us (42%)
  blocking collectives  171 us (24%)
  matrix products  80.2 us (11%)
  local copies, waits for them, and re-layouts  71.6 us (10%)
  starting transfers between devices  37.5 us (5%)
  other arithmetic  35.2 us (5%)
  between operations  15.1 us (2%)
    reduce_scatter x1, waiting for transfers between devices, local(): lax.psum_scatter(grad_qkv_part, ('fsdp', 'seq'), scatter_dimension=0, til...  125 us
    unnamed x2, blocking collectives  114 us
    reduce_scatter x1, waiting for transfers between devices, local(): lax.psum_scatter(grad_proj, ('fsdp', 'seq'), scatter_dimension=0, tiled=T...  70.7 us
    all_to_all x1, blocking collectives, local(): lax.all_to_all(stacked, 'seq', split_axis=0, concat_axis=2, tiled=True)  56.5 us
    all_gather x1, waiting for transfers between devices, local(): lax.all_gather(expert_up, 'seq', axis=2, tiled=True)  50.1 us
    all_gather x1, waiting for transfers between devices, local(): lax.all_gather(proj_weight, ('fsdp', 'seq'), axis=0, tiled=True)  25 us
    unnamed x70, local copies, waits for them, and re-layouts  15.7 us
  transfers between devices with their start and end apart: 17, of which 8 were waited for; matrix products, arithmetic and copies ran while one was open for 23% of the time, Pallas kernels for 0%

profile of v1, /device:TPU:0, one launch (start us, length us, event | category | flops | bytes accessed | tf_op | source)
XLA Modules:
  0.0 716.9 jit_solution(8244464965263804085)
XLA Ops:
  9.4 5.1 collective-permute-start.1
  19.0 74.9 %all-reduce.9 = (bf16[768]{0:T(1024)(128)(2,1)S(1)}, bf16[768]{0:T(1024)(128)(2,1)S(1)}, bf16[768]{0:T(1024)(128)(2,1)S(1)}, bf16[768]{0:T(1024)(128)(2,1)S(1)}) all-reduce(bf16[768]{0:T(1024)(128)(2,1)S(1)} %dynamic-update-slice.1, bf16[768]{0:T(1024)(128)(2,1)S(1)} %dynamic-update-slice, ...), channel_id=1, replica_groups=mesh['fsdp'=8,'seq'=4] {'fsdp','seq'}, use_global_device_ids=true, to_apply=%add.1 | all-reduce | flops 3072 | bytes 12288
  106.2 14.5 %all-to-all-done = bf16[128,3,4,192]{0,3,1,2:T(8,128)(2,1)S(1)} async-done(((bf16[128,3,4,192]{0,3,1,2:T(8,128)(2,1)}), bf16[128,3,4,192]{0,3,1,2:T(8,128)(2,1)S(1)}, u32[]{:S(2)}, u32[]{:S(2)}) %all-to-all-start) | async-done | bytes 589856 | tf_op jit(solution)/shard_map/all_to_all | solution.py:181
  146.1 25.0 %all-gather.6.cloned.1.call-done = bf16[768,768]{1,0:T(8,128)(2,1)} async-done(((bf16[24,768]{1,0:T(8,128)(2,1)}), bf16[768,768]{1,0:T(8,128)(2,1)}) %all-gather.6.cloned.1.call-update) | async-done | bytes 1179664 | tf_op jit(solution)/shard_map/all_gather | solution.py:169
  181.1 4.7 all-to-all-start.2
  203.0 4.2 all-to-all-start.4
  209.7 50.1 %all-gather.8.cloned.1.call-done = bf16[1,768,3072]{2,1,0:T(8,128)(2,1)} async-done(((bf16[1,768,768]{2,1,0:T(8,128)(2,1)}), bf16[1,768,3072]{2,1,0:T(8,128)(2,1)}) %all-gather.8.cloned.1.call-update) | async-done | bytes 4718608 | tf_op jit(solution)/shard_map/all_gather | solution.py:212
  259.8 7.9 %fusion.10 = f32[512,3072]{1,0:T(8,128)} fusion(bf16[512,768]{1,0:T(8,128)(2,1)} %bitcast.15, bf16[1,768,3072]{2,1,0:T(8,128)(2,1)} %all-gather.8.cloned.1.call-done), kind=kOutput, calls=%fused_computation.19 | convolution fusion | flops 2415919104 | bytes 11796480 | tf_op jit(solution)/shard_map/dot_general | solution.py:112
  267.6 8.5 %fusion.7 = bf16[512,3072]{1,0:T(8,128)(2,1)S(1)} fusion(f32[512,3072]{1,0:T(8,128)} %fusion.10, bf16[512,768]{1,0:T(8,128)(2,1)} %bitcast.24, bf16[768,3072]{1,0:T(8,128)(2,1)} %bitcast_dynamic-update-slice_fusion), kind=kOutput, calls=%fused_computation.13 | convolution fusion | flops 2447376384 | bytes 14942208 | tf_op jit(solution)/shard_map/dot_general | solution.py:121
  277.9 5.5 fusion.12
  283.7 8.1 %fusion.13 = bf16[1,768,3072]{2,1,0:T(8,128)(2,1)} fusion(bf16[512,768]{1,0:T(8,128)(2,1)} %bitcast.24, f32[512,3072]{1,0:T(8,128)} %fusion.10), kind=kOutput, calls=%fused_computation.22 | convolution fusion | flops 2432434176 | bytes 11796480 | tf_op jit(solution)/shard_map/dot_general | solution.py:124
  291.8 8.8 %convolution_convert_fusion.3 = bf16[512,768]{1,0:T(8,128)(2,1)} fusion(bf16[768,3072]{1,0:T(8,128)(2,1)} %bitcast_dynamic-update-slice_fusion, f32[512,3072]{1,0:T(8,128)} %fusion.10), kind=kOutput, calls=%fused_computation.40 | convolution fusion | flops 2430468096 | bytes 11796480 | tf_op jit(solution)/shard_map/dot_general | solution.py:114
  300.7 4.2 all-to-all-start.3
  304.9 6.8 fusion.29
  311.7 5.8 all-to-all-done.3
  317.5 4.2 all-to-all-start.5
  326.7 7.6 %all-to-all-done.5 = bf16[8,64,768]{2,1,0:T(8,128)(2,1)} async-done(((bf16[8,64,768]{2,1,0:T(8,128)(2,1)}), bf16[8,64,768]{2,1,0:T(8,128)(2,1)}, u32[]{:S(2)}, u32[]{:S(2)}) %all-to-all-start.5) | async-done | bytes 786464 | tf_op jit(solution)/shard_map/all_to_all | solution.py:141
  364.8 5.8 all-to-all-done.6
  381.7 5.2 fusion.36
  388.9 5.3 fusion.39
  398.7 56.5 %all_to_all.83 = bf16[512,3,1,192]{3,1,2,0:T(4,128)(2,1)S(1)} all-to-all(bf16[512,3,1,192]{3,1,2,0:T(4,128)(2,1)S(1)} %pad_maximum_fusion), channel_id=1, replica_groups=mesh['fsdp'=8,'seq'=4] {'seq'}, dimensions={0} | all-to-all | bytes 1179648 | tf_op jit(solution)/shard_map/all_to_all | solution.py:260
  465.4 39.5 %all-reduce.8 = (f32[768]{0:T(1024)S(1)}, f32[768]{0:T(1024)S(1)}, f32[768]{0:T(1024)S(1)}, f32[768]{0:T(1024)S(1)}) all-reduce(f32[768]{0:T(1024)S(1)} %get-tuple-element.48, f32[768]{0:T(1024)S(1)} %get-tuple-element.50, f32[768]{0:T(1024)S(1)} %copy-done.15, ...), channel_id=4, replica_groups=mesh['fsdp'=8,'seq'=4] {'fsdp','seq'}, use_global_device_ids=true, to_apply=%region_23.24.clone | all-reduce | flops 3072 | bytes 24576
  514.0 70.7 %reduce-scatter.7.cloned.1.call-done = f32[24,768]{1,0:T(8,128)} async-done(((f32[768,768]{1,0:T(8,128)}), f32[24,768]{1,0:T(8,128)}) %reduce-scatter.7.cloned.1.call-update) | async-done | bytes 73744 | tf_op jit(solution)/shard_map/reduce_scatter | solution.py:274
  584.7 124.9 %reduce-scatter.5.cloned.1.call-done = f32[24,2304]{1,0:T(8,128)} async-done(((f32[768,2304]{1,0:T(8,128)}), f32[24,2304]{1,0:T(8,128)}) %reduce-scatter.5.cloned.1.call-update) | async-done | bytes 221200 | tf_op jit(solution)/shard_map/reduce_scatter | solution.py:273
  (187 shorter events, 148.1 us)
Async XLA Ops:
  7.2 89.0 %all-gather.4.cloned.1.call-start = ((), (), s32[]{:S(2)}) async-start(), calls=%async_computation.12 | async-start | bytes 3649536 | tf_op jit(solution)/shard_map/all_gather | solution.py:168
  7.9 163.2 %all-gather.6.cloned.1.call-start = ((), (), s32[]{:S(2)}) async-start(), calls=%async_computation.13 | async-start | bytes 1216512 | tf_op jit(solution)/shard_map/all_gather | solution.py:169
  8.7 251.1 %all-gather.8.cloned.1.call-start = ((), (), s32[]{:S(2)}) async-start(), calls=%async_computation.14 | async-start | bytes 5898240 | tf_op jit(solution)/shard_map/all_gather | solution.py:212
  9.4 191.1 %collective-permute-start.1 = (bf16[1,768,768]{2,1,0:T(8,128)(2,1)}, bf16[1,768,768]{2,1,0:T(8,128)(2,1)}, u32[]{:S(2)}, u32[]{:S(2)}) collective-permute-start(bf16[1,768,768]{2,1,0:T(8,128)(2,1)} %param.20), channel_id=1, source_target_pairs={{0,3},{1,0},{2,1},{3,2},{4,7},{5,4},{6,5},{7,6},{8,11},{9,8},{10,9... | collective-permute-start | bytes 3538952 | tf_op jit(solution)/shard_map/ppermute | solution.py:24
  14.5 122.5 %collective-permute-start = (bf16[1,768,768]{2,1,0:T(8,128)(2,1)}, bf16[1,768,768]{2,1,0:T(8,128)(2,1)}, u32[]{:S(2)}, u32[]{:S(2)}) collective-permute-start(bf16[1,768,768]{2,1,0:T(8,128)(2,1)} %param.20), channel_id=1, source_target_pairs={{0,1},{1,2},{2,3},{3,0},{4,5},{5,6},{6,7},{7,4},{8,9},{9,10},{10,1... | collective-permute-start | bytes 3538952 | tf_op jit(solution)/shard_map/ppermute | solution.py:19
  96.2 9.3 %copy-start.18 = (f32[128,2]{0,1:T(2,128)S(1)}, f32[128,2]{0,1:T(2,128)}, u32[]{:S(2)}) copy-start(f32[128,2]{0,1:T(2,128)} %param.21) | copy-start | bytes 3076
  100.2 20.5 %all-to-all-start = ((bf16[128,3,4,192]{0,3,1,2:T(8,128)(2,1)}), bf16[128,3,4,192]{0,3,1,2:T(8,128)(2,1)S(1)}, u32[]{:S(2)}, u32[]{:S(2)}) async-start(bf16[128,3,4,192]{0,3,1,2:T(8,128)(2,1)} %copy.60), calls=%async_computation | async-start | bytes 1179648 | tf_op jit(solution)/shard_map/all_to_all | solution.py:181
  105.5 25.9 %copy-start.20 = (f32[128]{0:T(128)}, f32[128]{0:T(128)S(1)}, u32[]{:S(2)}) copy-start(f32[128]{0:T(128)S(1)} %reduce_max.20) | copy-start | bytes 1540
  127.4 11.6 %all-to-all-start.1 = ((bf16[4,2,12288]{2,1,0:T(2,128)(2,1)}), bf16[4,2,12288]{2,1,0:T(2,128)(2,1)}, u32[]{:S(2)}, u32[]{:S(2)}) async-start(bf16[4,2,12288]{2,1,0:T(2,128)(2,1)} %reshape.283), calls=%async_computation.1 | async-start | bytes 393216 | tf_op jit(solution)/shard_map/all_to_all | solution.py:192
  135.9 35.3 %copy-start = (f32[128,768]{1,0:T(8,128)S(1)}, f32[128,768]{1,0:T(8,128)}, u32[]{:S(2)}) copy-start(f32[128,768]{1,0:T(8,128)} %param.12) | copy-start | bytes 1179652
  137.0 70.2 %collective-permute-start.2 = (bf16[1,768,768]{2,1,0:T(8,128)(2,1)}, bf16[1,768,768]{2,1,0:T(8,128)(2,1)}, u32[]{:S(2)}, u32[]{:S(2)}) collective-permute-start(bf16[1,768,768]{2,1,0:T(8,128)(2,1)} %collective-permute-done), channel_id=1, source_target_pairs={{0,1},{1,2},{2,3},{3,0},{4,5},{5,6},{6,7},{7,4},{8,9},{9,10},{10,1... | collective-permute-start | bytes 3538952 | tf_op jit(solution)/shard_map/ppermute | solution.py:19
  181.1 21.9 %all-to-all-start.2 = ((bf16[8,64,768]{2,1,0:T(8,128)(2,1)}), bf16[8,64,768]{2,1,0:T(8,128)(2,1)}, u32[]{:S(2)}, u32[]{:S(2)}) async-start(bf16[8,64,768]{2,1,0:T(8,128)(2,1)} %bitcast.103), calls=%async_computation.2 | async-start | bytes 1572864 | tf_op jit(solution)/shard_map/all_to_all | solution.py:137
  203.0 64.7 %all-to-all-start.4 = ((bf16[8,64,768]{2,1,0:T(8,128)(2,1)}), bf16[8,64,768]{2,1,0:T(8,128)(2,1)}, u32[]{:S(2)}, u32[]{:S(2)}) async-start(bf16[8,64,768]{2,1,0:T(8,128)(2,1)} %bitcast.104), calls=%async_computation.4 | async-start | bytes 1572864 | tf_op jit(solution)/shard_map/all_to_all | solution.py:137
  207.2 301.1 %reduce-scatter.9.cloned.1.call-start = ((), (), s32[]{:S(2)}) async-start(), calls=%async_computation.17 | async-start | bytes 5898240 | tf_op jit(solution)/shard_map/reduce_scatter | solution.py:223
  283.5 227.7 %reduce-scatter.11.cloned.1.call-start = ((), (), s32[]{:S(2)}) async-start(), calls=%async_computation.18 | async-start | bytes 5898240 | tf_op jit(solution)/shard_map/reduce_scatter | solution.py:226
  300.7 16.8 %all-to-all-start.3 = ((bf16[8,64,768]{2,1,0:T(8,128)(2,1)}), bf16[8,64,768]{2,1,0:T(8,128)(2,1)}, u32[]{:S(2)}, u32[]{:S(2)}) async-start(bf16[8,64,768]{2,1,0:T(8,128)(2,1)} %bitcast.116), calls=%async_computation.3 | async-start | bytes 1572864 | tf_op jit(solution)/shard_map/all_to_all | solution.py:141
  317.5 16.8 %all-to-all-start.5 = ((bf16[8,64,768]{2,1,0:T(8,128)(2,1)}), bf16[8,64,768]{2,1,0:T(8,128)(2,1)}, u32[]{:S(2)}, u32[]{:S(2)}) async-start(bf16[8,64,768]{2,1,0:T(8,128)(2,1)} %bitcast.115), calls=%async_computation.5 | async-start | bytes 1572864 | tf_op jit(solution)/shard_map/all_to_all | solution.py:141
  321.7 263.0 %reduce-scatter.7.cloned.1.call-start = ((), (), s32[]{:S(2)}) async-start(), calls=%async_computation.16 | async-start | bytes 2433024 | tf_op jit(solution)/shard_map/reduce_scatter | solution.py:274
  359.2 11.4 %all-to-all-start.6 = ((bf16[128,4,192]{0,2,1:T(8,128)(2,1)}), bf16[128,4,192]{0,2,1:T(8,128)(2,1)}, u32[]{:S(2)}, u32[]{:S(2)}) async-start(bf16[128,4,192]{0,2,1:T(8,128)(2,1)} %bitcast.117), calls=%async_computation.6 | async-start | bytes 393216 | tf_op jit(solution)/shard_map/all_to_all | solution.py:251
  363.2 346.4 %reduce-scatter.5.cloned.1.call-start = ((), (), s32[]{:S(2)}) async-start(), calls=%async_computation.15 | async-start | bytes 7299072 | tf_op jit(solution)/shard_map/reduce_scatter | solution.py:273
  395.4 61.2 %copy-start.14 = (f32[128]{0:T(128)S(1)}, f32[128]{0:T(128)}, u32[]{:S(2)}) copy-start(f32[128]{0:T(128)} %copy-done.13) | copy-start | bytes 1540
  395.5 61.2 %copy-start.17 = (f32[128]{0:T(128)S(1)}, f32[128]{0:T(128)}, u32[]{:S(2)}) copy-start(f32[128]{0:T(128)} %copy-done.16) | copy-start | bytes 1540
  460.8 46.4 %copy-start.24 = (f32[128]{0:T(128)S(1)}, f32[128]{0:T(128)}, u32[]{:S(2)}) copy-start(f32[128]{0:T(128)} %copy-done.23) | copy-start | bytes 1540
  461.8 45.6 %copy-start.3 = (f32[128,768]{1,0:T(8,128)S(1)}, f32[128,768]{1,0:T(8,128)}, u32[]{:S(2)}) copy-start(f32[128,768]{1,0:T(8,128)} %copy-done.2) | copy-start | bytes 1179652
  (20 other events, 62.1 us)
Sparse Core Ops, SparseCore 0:
  10.8 84.1 all-gather.3
  97.8 73.3 all-gather.5
  172.7 86.9 all-gather.7
  283.6 84.6 reduce-scatter.8
  370.5 104.1 reduce-scatter.10
  480.4 104.2 reduce-scatter.6
  590.9 118.5 reduce-scatter.4
